TPU v7x, 256 devices: a whole 4x4x8 slice. The times are simulated.
256 devices in a mesh: dp: 16 (over y, z_hi), ctx: 16 (over x, z_lo, core).
Axes of the slice: x: 4, y: 4, z: 8 (z_hi: 4, z_lo: 2; z = z_hi * 2 + z_lo), core: 2. Of those that a mesh axis runs over, the one named last changes fastest.
Arguments:
- route_pos: int32 [16, 2048], P('dp', 'ctx'), may hold values from -1 to 8191, as said below
- x_routed: bfloat16 [16, 2048, 4096], P('dp', 'ctx'), may hold values from -6 to 6
- w_router: bfloat16 [4096], P('dp'), may hold values from -0.09375 to 0.09375
- queries: bfloat16 [16, 2048, 2048], P('dp', 'ctx'), may hold values from -8 to 8
- keys: bfloat16 [16, 2048, 2048], P('dp', 'ctx'), may hold values from -8 to 8
- values: bfloat16 [16, 2048, 2048], P('dp', 'ctx'), may hold values from -6 to 6
- d_gated: float32 [16, 2048, 2048], P('dp', 'ctx'), may hold values from -6 to 6
Outputs:
- grad_queries: float32 [16, 2048, 2048], P('dp', 'ctx')
- grad_keys: float32 [16, 2048, 2048], P('dp', 'ctx')
- grad_values: float32 [16, 2048, 2048], P('dp', 'ctx')
- router_grad: float32 [4096], P('dp')
Inputs may be any that keep to these rules, and one draw needn't show every extreme that they name: `route_pos`: in each sequence, context shard c lists in its 128 slots the increasing positions of its routed tokens, all from c * 512 to (c + 1) * 512 - 1, then -1 in its unused slots. A shard holds 0 to 128 routed tokens and a sequence 1024 in all; in every sequence some shard holds exactly 128 and some shard none.
All inputs are finite; a program needn't handle non-finite values.
Results may differ from a plain program's by a relative error of at most 0.017.
Values may be sent and summed in bfloat16 or wider, within the bound.
A program may use at most 128 MiB of HBM per device.

v0:
```python
import jax
import jax.numpy as jnp
from jax import lax
from jax.sharding import PartitionSpec as P

HEAD = 128


NEG_FILL = -1e30


def laid_out(parts, dim):
    parts = jnp.moveaxis(parts, 0, dim)
    shape = parts.shape
    return parts.reshape(*shape[:dim], shape[dim] * shape[dim + 1], *shape[dim + 2 :])


def sent_to_all(array, axis):
    copies = jnp.broadcast_to(array, (lax.axis_size(axis), *array.shape))
    return lax.all_to_all(copies, axis, split_axis=0, concat_axis=0, tiled=True)


def gathered_copies(array, axis, dim):
    return laid_out(sent_to_all(array, axis), dim)


def in_one_piece(arrays, axis, dim, along):
    ends, at = ([], 0)
    for a in arrays[:-1]:
        at += a.shape[along]
        ends.append(at)
    both = jnp.concatenate(arrays, axis=along)
    return tuple(jnp.split(lax.all_gather(both, axis, axis=dim, tiled=True), ends, axis=along))


def over_copies(array, axis):
    everything = sent_to_all(array, axis)
    return jnp.sum(everything, axis=0)


def in_blocks(array, dim, devices):
    shape = array.shape
    parts = array.reshape(*shape[:dim], devices, shape[dim] // devices, *shape[dim + 1 :])
    return jnp.moveaxis(parts, dim, 0)


def summed_on_arrival(array, axis, dim):
    devices = lax.axis_size(axis)
    parts = lax.all_to_all(in_blocks(array, dim, devices), axis, 0, 0, tiled=True)
    return jnp.sum(parts, axis=0)


def body(route_pos, x_routed, w_router, queries, keys, values, d_gated):
    slot_count = queries.shape[1]
    width = queries.shape[2]
    head_count = width // HEAD
    score_scale = HEAD ** (-0.5)
    positions = route_pos[0]
    is_live = positions >= 0
    live_float = is_live.astype(jnp.float32)
    router_full = gathered_copies(w_router, "dp", 0)
    router_logit = jnp.dot(x_routed[0], router_full, preferred_element_type=jnp.float32)
    gate_value = jax.nn.sigmoid(router_logit)
    grad_rows = d_gated[0]
    grad_out = ((gate_value * live_float)[:, None] * grad_rows).astype(jnp.bfloat16)
    key_all, value_all, key_positions = (
        *in_one_piece((keys, values), "ctx", 1, 0),
        lax.all_gather(route_pos, "ctx", axis=1, tiled=True),
    )
    query_heads = queries[0].reshape(slot_count, head_count, HEAD)
    grad_heads = grad_out.reshape(slot_count, head_count, HEAD)
    key_heads = key_all[0].reshape(-1, head_count, HEAD)
    value_heads = value_all[0].reshape(-1, head_count, HEAD)
    key_pos = key_positions[0]
    allowed = is_live[:, None] & (key_pos >= 0)[None, :] & (key_pos[None, :] <= positions[:, None])
    scores = (
        jnp.einsum("qhd,khd->hqk", query_heads, key_heads, preferred_element_type=jnp.float32)
        * score_scale
    )
    scores = jnp.where(allowed[None], scores, NEG_FILL)
    row_max = jnp.max(scores, axis=-1, keepdims=True)
    exponent = jnp.exp(scores - row_max)
    row_total = jnp.sum(exponent, axis=-1, keepdims=True)
    weights = exponent / row_total
    weights_low = weights.astype(jnp.bfloat16)
    attended = jnp.einsum(
        "hqk,khd->qhd", weights_low, value_heads, preferred_element_type=jnp.float32
    )
    grad_weights = jnp.einsum(
        "qhd,khd->hqk", grad_heads, value_heads, preferred_element_type=jnp.float32
    )
    row_delta = jnp.sum(grad_heads.astype(jnp.float32) * attended, axis=-1)
    grad_scores = weights * (grad_weights - row_delta.T[:, :, None]) * score_scale
    grad_low = grad_scores.astype(jnp.bfloat16)
    grad_query = jnp.einsum("hqk,khd->qhd", grad_low, key_heads, preferred_element_type=jnp.float32)
    grad_query = grad_query.reshape(slot_count, width)
    grad_gate = jnp.sum(attended.reshape(slot_count, width) * grad_rows, axis=-1) * live_float
    grad_logit = grad_gate * gate_value * (1.0 - gate_value)
    router_term = jnp.dot(
        grad_logit, x_routed[0].astype(jnp.float32), precision=lax.Precision.HIGHEST
    )
    total_routed = float(lax.axis_size("dp") * lax.axis_size("ctx") * slot_count // 2)
    window_sum = over_copies(router_term, "ctx")
    router_grad = summed_on_arrival(window_sum, "dp", 0)
    router_grad = router_grad / total_routed
    stats_all = in_one_piece(
        (row_max[:, :, 0].T[None], row_total[:, :, 0].T[None], row_delta[None]), "ctx", 1, 0
    )
    own_keys = keys[0].reshape(slot_count, head_count, HEAD)
    own_values = values[0].reshape(slot_count, head_count, HEAD)
    piece_queries, piece_grads, piece_positions = (
        *in_one_piece((queries, grad_out[None]), "ctx", 1, 0),
        lax.all_gather(route_pos, "ctx", axis=1, tiled=True),
    )
    row_span = piece_queries.shape[1]
    groups = row_span // slot_count
    query_group = piece_queries[0].reshape(groups, slot_count, head_count, HEAD)
    grad_group = piece_grads[0].reshape(groups, slot_count, head_count, HEAD)
    pos_group = piece_positions[0].reshape(groups, slot_count)

    def stat_group(stat_rows):
        picked = stat_rows[0]
        return jnp.transpose(picked.reshape(groups, slot_count, head_count), (0, 2, 1))[..., None]

    group_max = stat_group(stats_all[0])
    group_total = stat_group(stats_all[1])
    group_delta = stat_group(stats_all[2])
    mask_group = (
        (pos_group >= 0)[:, :, None]
        & is_live[None, None, :]
        & (positions[None, None, :] <= pos_group[:, :, None])
    )
    local_scores = (
        jnp.einsum("nqhd,khd->nhqk", query_group, own_keys, preferred_element_type=jnp.float32)
        * score_scale
    )
    local_scores = jnp.where(mask_group[:, None], local_scores, NEG_FILL)
    local_weights = jnp.exp(local_scores - group_max) / group_total
    local_low = local_weights.astype(jnp.bfloat16)
    local_dweights = jnp.einsum(
        "nqhd,khd->nhqk", grad_group, own_values, preferred_element_type=jnp.float32
    )
    local_grad = (local_weights * (local_dweights - group_delta) * score_scale).astype(jnp.bfloat16)
    key_part = jnp.einsum(
        "nhqk,nqhd->nkhd", local_grad, query_group, preferred_element_type=jnp.float32
    )
    value_part = jnp.einsum(
        "nhqk,nqhd->nkhd", local_low, grad_group, preferred_element_type=jnp.float32
    )
    key_part = lax.optimization_barrier(key_part.astype(jnp.bfloat16)).astype(jnp.float32)
    value_part = lax.optimization_barrier(value_part.astype(jnp.bfloat16)).astype(jnp.float32)
    grad_key = jnp.sum(key_part, axis=0).reshape(slot_count, width)
    grad_value = jnp.sum(value_part, axis=0).reshape(slot_count, width)
    return (grad_query[None], grad_key[None], grad_value[None], router_grad)


def solution(mesh):
    placed = (
        P("dp", "ctx"),
        P("dp", "ctx", None),
        P("dp"),
        P("dp", "ctx", None),
        P("dp", "ctx", None),
        P("dp", "ctx", None),
        P("dp", "ctx", None),
    )
    return jax.shard_map(
        body,
        mesh=mesh,
        in_specs=placed,
        out_specs=(P("dp", "ctx", None), P("dp", "ctx", None), P("dp", "ctx", None), P("dp")),
        check_vma=False,
    )
```

profile of v0, /device:TPU:1, one launch (start us, length us, event | category | flops | bytes accessed | tf_op | source)
XLA Modules:
  0.0 317.7 jit_solution(9462035267026638578)
XLA Ops:
  7.2 1.4 copy.105
  8.6 1.3 copy.104
  9.9 1.1 pad_maximum_fusion
  11.0 0.0 all-gather.5.cloned.1.call-start
  11.1 0.7 broadcast_in_dim.55
  11.8 0.5 broadcast.144
  12.3 0.7 reduce.5
  13.0 20.4 %all_to_all.21 = bf16[16,2,128]{2,1,0:T(2,128)(2,1)S(1)} all-to-all(bf16[16,2,128]{2,1,0:T(2,128)(2,1)S(1)} %reshape.133), channel_id=1, replica_groups=mesh['dp'=16,'ctx'=16] {'dp'}, dimensions={0} | all-to-all | bytes 16384 | tf_op jit(solution)/shard_map/all_to_all | solution.py:20
  33.4 1.0 broadcast_select_fusion
  34.4 1.4 multiply_convert_fusion.2
  35.8 2.1 pad_maximum_fusion.1
  37.9 1.6 copy.108
  39.5 1.1 copy.142
  40.6 2.1 copy.144
  42.7 2.0 copy.148
  44.7 21.4 %all_gather.16 = s32[1,2048]{1,0:T(1,128)S(1)} all-gather(s32[1,128]{1,0:T(1,128)} %param.7), channel_id=1, replica_groups=mesh['dp'=16,'ctx'=16] {'ctx'}, dimensions={1}, use_global_device_ids=true | all-gather | bytes 8704 | tf_op jit(solution)/shard_map/all_gather | solution.py:68
  66.2 0.7 broadcast_compare_fusion.1
  66.8 2.0 compare_and_fusion
  68.8 2.1 compare_and_fusion.1
  70.9 44.9 %all-gather.3.cloned.1.call-done = bf16[2,2048,2048]{1,2,0:T(8,128)(2,1)} async-done(((bf16[2,128,2048]{1,2,0:T(8,128)(2,1)}), bf16[2,2048,2048]{1,2,0:T(8,128)(2,1)}) %all-gather.3.cloned.1.call-update) | async-done | bytes 16777232 | tf_op jit(solution)/shard_map/all_gather | solution.py:33
  115.8 12.1 %fusion.60 = (bf16[1,2048,2048]{1,2,0:T(8,128)(2,1)}, bf16[1,2048,2048]{1,2,0:T(8,128)(2,1)}) fusion(bf16[2,2048,2048]{1,2,0:T(8,128)(2,1)} %all-gather.3.cloned.1.call-done), kind=kLoop, calls=%fused_computation.76 | loop fusion | bytes 33554432 | tf_op jit(solution)/shard_map/split | solution.py:33
  127.9 13.9 %fusion.7 = (f32[16,128]{1,0:T(8,128)S(1)}, f32[16,2048,128]{2,1,0:T(8,128)}) fusion(pred[128,2048]{0,1:T(8,128)(4,1)S(1)} %compare_and_fusion.1, bf16[2048,16,128]{0,2,1:T(8,128)(2,1)} %bitcast.142, bf16[128,16,128]{2,1,0:T(8,128)(2,1)S(1)} %bitcast.149), kind=kOutput, calls=%fused_computation.14 | convolution fusion | flops 1086322688 | bytes 25960448 | tf_op jit(solution)/shard_map/qhd,khd->hqk/dot_general | solution.py:77
  141.8 9.4 %fusion.6 = f32[16,128]{1,0:T(8,128)S(1)} fusion(f32[16,2048,128]{2,1,0:T(8,128)} %get-tuple-element.38, f32[16,128]{1,0:T(8,128)S(1)} %get-tuple-element.37, pred[128,2048]{0,1:T(8,128)(4,1)S(1)} %compare_and_fusion.1), kind=kLoop, calls=%fused_computation.13 | loop fusion | flops 16775168 | bytes 17055744 | tf_op jit(solution)/shard_map/reduce_sum | solution.py:83
  151.3 14.8 %multiply_reduce_fusion = (f32[128]{0:T(128)S(1)}, f32[128,16]{0,1:T(8,128)S(1)}) fusion(f32[128,16,128]{0,2,1:T(8,128)S(1)} %bitcast.153, f32[128]{0:T(128)S(1)} %get-tuple-element.39, bf16[2048,16,128]{0,2,1:T(8,128)(2,1)} %bitcast.144, f32[16,128]{1,0:T(8,128)S(1)} %fusion.6, f32[16,128]{1,0:T(8,128)S(1)} %get-tuple-element.37, ...), kind=kOutput, calls=%fused_computation.44 | convolution fusion | flops 1096546176 | bytes 26502144 | tf_op jit(solution)/shard_map/hqk,khd->qhd/dot_general | solution.py:86
  166.1 16.9 %fusion.8 = f32[16,128,128]{2,1,0:T(8,128)} fusion(bf16[2048,16,128]{0,2,1:T(8,128)(2,1)} %bitcast.143, f32[16,128]{1,0:T(8,128)S(1)} %bitcast.169, bf16[2048,16,128]{0,2,1:T(8,128)(2,1)} %bitcast.145, f32[16,2048,128]{2,1,0:T(8,128)} %get-tuple-element.38, f32[16,128]{1,0:T(8,128)S(1)} %fusion.6, f32[16,128]{1,0:T(8,128)S(1)} %get-tuple-element.37, ...), kind=kOutput, calls=%fused_computation.15 | convolution fusion | flops 2181562368 | bytes 35938816 | tf_op jit(solution)/shard_map/hqk,khd->qhd/dot_general | solution.py:95
  183.0 2.5 copy.125
  185.5 22.2 %all_gather.19 = f32[3,2048,16]{1,2,0:T(8,128)S(1)} all-gather(f32[3,128,16]{1,2,0:T(8,128)S(1)} %pad_maximum_fusion.2), channel_id=1, replica_groups=mesh['dp'=16,'ctx'=16] {'ctx'}, dimensions={1}, use_global_device_ids=true | all-gather | bytes 417792 | tf_op jit(solution)/shard_map/all_gather | solution.py:33
  207.7 0.7 copy.146
  208.4 0.7 copy.145
  209.1 0.5 fusion.40
  209.6 0.9 broadcast_in_dim.61
  210.5 3.7 %all-to-all-start.1 = ((f32[16,1,4096]{2,1,0:T(1,128)}), f32[16,1,4096]{2,1,0:T(1,128)S(1)}, u32[]{:S(2)}, u32[]{:S(2)}) async-start(f32[16,1,4096]{2,1,0:T(1,128)} %broadcast_in_dim.61), calls=%async_computation.1 | async-start | bytes 524288 | tf_op jit(solution)/shard_map/all_to_all | solution.py:20
  214.3 1.3 all-gather.5.cloned.1.call-done
  215.6 11.8 %slice_bitcast_fusion = (bf16[256,8,16,128]{3,1,2,0:T(8,128)(2,1)}, bf16[256,8,16,128]{3,1,2,0:T(8,128)(2,1)}) fusion(bf16[2,2048,2048]{2,1,0:T(8,128)(2,1)} %all-gather.5.cloned.1.call-done), kind=kLoop, calls=%fused_computation.16 | loop fusion | bytes 33554432
  227.4 9.8 %copy.143 = bf16[256,8,16,128]{3,2,1,0:T(8,128)(2,1)} copy(bf16[256,8,16,128]{3,1,2,0:T(8,128)(2,1)} %get-tuple-element.31) | data formatting | bytes 16777216
  237.3 9.8 %copy.147 = bf16[256,8,16,128]{3,2,1,0:T(8,128)(2,1)} copy(bf16[256,8,16,128]{3,1,2,0:T(8,128)(2,1)} %get-tuple-element.30) | data formatting | bytes 16777216
  247.1 14.2 %fusion.61 = (bf16[16,16,128,128]{3,2,0,1:T(8,128)(2,1)}, f32[16,16,128,128]{3,2,0,1:T(8,128)S(1)}) fusion(f32[16,16,128]{2,0,1:T(8,128)S(1)} %bitcast.161, f32[16,16,128]{2,0,1:T(8,128)S(1)} %bitcast.162, bf16[128,16,128,1]{2,1,0,3:T(8,128)(2,1)S(1)} %bitcast.157, bf16[16,128,16,128]{3,2,1,0:T(8,128)(2,1)} %bitcast.140, pred[16,128,128]{2,1,0:T(8,128)(4,1)S(1)} %copy-done.5), kind=kOutput, calls=%fused_computation.77 | convolution fusion | flops 1094713344 | bytes 34603008 | tf_op jit(solution)/shard_map/nqhd,khd->nhqk/dot_general | solution.py:134
  261.3 8.4 %fusion.2 = bf16[16,16,128,128]{3,2,0,1:T(8,128)(2,1)} fusion(f32[16,16,128,128]{3,2,0,1:T(8,128)S(1)} %get-tuple-element.42, bf16[16,128,16,128]{3,2,1,0:T(8,128)(2,1)S(1)} %bitcast.138, f32[16,16,128]{2,0,1:T(8,128)S(1)} %bitcast.156, bf16[128,16,128,1]{2,1,0,3:T(8,128)(2,1)S(1)} %bitcast.148), kind=kOutput, calls=%fused_computation.3 | convolution fusion | flops 1090519040 | bytes 34209792 | tf_op jit(solution)/shard_map/nqhd,khd->nhqk/dot_general | solution.py:140
  269.7 9.6 %convert_bitcast_fusion.1 = bf16[16,128,16,128]{1,3,2,0:T(8,128)(2,1)} fusion(bf16[16,16,128,128]{3,2,0,1:T(8,128)(2,1)} %fusion.2, bf16[16,128,16,128]{3,2,1,0:T(8,128)(2,1)} %bitcast.141), kind=kOutput, calls=%fused_computation.27 | convolution fusion | flops 1077936128 | bytes 25165824 | tf_op jit(solution)/shard_map/nhqk,nqhd->nkhd/dot_general | solution.py:144
  279.4 7.5 %convert_bitcast_fusion = bf16[16,128,16,128]{1,3,2,0:T(8,128)(2,1)} fusion(bf16[16,16,128,128]{3,2,0,1:T(8,128)(2,1)} %get-tuple-element.41, bf16[16,128,16,128]{3,2,1,0:T(8,128)(2,1)S(1)} %bitcast.139), kind=kOutput, calls=%fused_computation.26 | convolution fusion | flops 1077936128 | bytes 25165824 | tf_op jit(solution)/shard_map/nhqk,nqhd->nkhd/dot_general | solution.py:147
  286.9 5.3 %convert_reduce_fusion.1 = f32[128,16,128]{0,2,1:T(8,128)S(1)} fusion(bf16[16,128,16,128]{1,3,2,0:T(8,128)(2,1)} %convert_bitcast_fusion.1), kind=kLoop, calls=%fused_computation.9 | loop fusion | flops 8126464 | bytes 9437184 | tf_op jit(solution)/shard_map/reduce_sum | solution.py:152
  292.2 0.8 reduce_sum.68
  293.0 8.4 %all-to-all-start.2 = ((f32[16,1,256]{2,1,0:T(1,128)}), f32[16,1,256]{2,1,0:T(1,128)S(1)}, u32[]{:S(2)}, u32[]{:S(2)}) async-start(f32[16,1,256]{2,1,0:T(1,128)} %bitcast.31), calls=%async_computation.2 | async-start | bytes 32768 | tf_op jit(solution)/shard_map/all_to_all | solution.py:49
  301.4 5.3 %convert_reduce_fusion = f32[128,16,128]{0,2,1:T(8,128)S(1)} fusion(bf16[16,128,16,128]{1,3,2,0:T(8,128)(2,1)} %convert_bitcast_fusion), kind=kLoop, calls=%fused_computation.8 | loop fusion | flops 8126464 | bytes 9437184 | tf_op jit(solution)/shard_map/reduce_sum | solution.py:153
  306.7 1.3 copy.126
  308.0 1.3 copy.127
  309.3 0.8 all-to-all-done.2
  310.1 0.6 broadcast_multiply_fusion
  (30 shorter events, 0.3 us)
Async XLA Ops:
  7.2 26.2 %copy-start = (bf16[1,128,4096]{2,1,0:T(8,128)(2,1)S(1)}, bf16[1,128,4096]{2,1,0:T(8,128)(2,1)}, u32[]{:S(2)}) copy-start(bf16[1,128,4096]{2,1,0:T(8,128)(2,1)} %param.8) | copy-start | bytes 3145732
  7.2 108.6 %all-gather.3.cloned.1.call-start = ((), (), s32[]{:S(2)}) async-start(), calls=%async_computation.3 | async-start | bytes 17825792 | tf_op jit(solution)/shard_map/all_gather | solution.py:33
  11.0 204.5 %all-gather.5.cloned.1.call-start = ((), (), s32[]{:S(2)}) async-start(), calls=%async_computation.4 | async-start | bytes 17825792 | tf_op jit(solution)/shard_map/all_gather | solution.py:33
  166.1 43.0 %copy-start.8 = (s32[1,128]{1,0:T(1,128)S(1)}, s32[1,128]{1,0:T(1,128)}, u32[]{:S(2)}) copy-start(s32[1,128]{1,0:T(1,128)} %param.7) | copy-start | bytes 1540
  210.5 81.7 %all-to-all-start.1 = ((f32[16,1,4096]{2,1,0:T(1,128)}), f32[16,1,4096]{2,1,0:T(1,128)S(1)}, u32[]{:S(2)}, u32[]{:S(2)}) async-start(f32[16,1,4096]{2,1,0:T(1,128)} %broadcast_in_dim.61), calls=%async_computation.1 | async-start | bytes 524288 | tf_op jit(solution)/shard_map/all_to_all | solution.py:20
  227.4 19.6 %copy-start.4 = (bf16[16,8,16,128]{3,2,1,0:T(8,128)(2,1)S(1)}, bf16[16,8,16,128]{3,2,1,0:T(8,128)(2,1)}, u32[]{:S(2)}) copy-start(bf16[16,8,16,128]{3,2,1,0:T(8,128)(2,1)} %copy.144) | copy-start | bytes 1572868
  227.4 19.6 %copy-start.5 = (pred[16,128,128]{2,1,0:T(8,128)(4,1)S(1)}, pred[16,128,128]{2,1,0:T(8,128)(4,1)}, u32[]{:S(2)}) copy-start(pred[16,128,128]{2,1,0:T(8,128)(4,1)} %compare_and_fusion) | copy-start | bytes 786436
  227.4 19.6 %copy-start.6 = (f32[2,8,16,128]{3,2,1,0:T(8,128)S(1)}, f32[2,8,16,128]{3,2,1,0:T(8,128)}, u32[]{:S(2)}) copy-start(f32[2,8,16,128]{3,2,1,0:T(8,128)} %copy.146) | copy-start | bytes 393220
  227.4 19.6 %copy-start.7 = (f32[2,8,16,128]{3,2,1,0:T(8,128)S(1)}, f32[2,8,16,128]{3,2,1,0:T(8,128)}, u32[]{:S(2)}) copy-start(f32[2,8,16,128]{3,2,1,0:T(8,128)} %copy.145) | copy-start | bytes 393220
  247.0 14.2 %copy-start.2 = (bf16[256,8,16,128]{3,2,1,0:T(8,128)(2,1)S(1)}, bf16[256,8,16,128]{3,2,1,0:T(8,128)(2,1)}, u32[]{:S(2)}) copy-start(bf16[256,8,16,128]{3,2,1,0:T(8,128)(2,1)} %copy.147) | copy-start | bytes 25165828
  247.1 14.2 %copy-start.3 = (bf16[16,8,16,128]{3,2,1,0:T(8,128)(2,1)S(1)}, bf16[16,8,16,128]{3,2,1,0:T(8,128)(2,1)}, u32[]{:S(2)}) copy-start(bf16[16,8,16,128]{3,2,1,0:T(8,128)(2,1)} %copy.148) | copy-start | bytes 1572868
  279.4 31.3 %copy-start.1 = (bf16[1,128,4096]{2,1,0:T(8,128)(2,1)S(1)}, bf16[1,128,4096]{2,1,0:T(8,128)(2,1)}, u32[]{:S(2)}) copy-start(bf16[1,128,4096]{2,1,0:T(8,128)(2,1)} %param.8) | copy-start | bytes 3145732
  293.0 17.1 %all-to-all-start.2 = ((f32[16,1,256]{2,1,0:T(1,128)}), f32[16,1,256]{2,1,0:T(1,128)S(1)}, u32[]{:S(2)}, u32[]{:S(2)}) async-start(f32[16,1,256]{2,1,0:T(1,128)} %bitcast.31), calls=%async_computation.2 | async-start | bytes 32768 | tf_op jit(solution)/shard_map/all_to_all | solution.py:49
Sparse Core Ops, SparseCore 0:
  11.2 104.6 all-gather.2
  118.2 97.3 all-gather.4
where the time goes:
time: 322 us; the launch traced here: 318 us
  matrix products  87 us (27%)
  blocking collectives  64 us (20%)
  local copies, waits for them, and re-layouts  61.7 us (19%)
  waiting for transfers between devices  47 us (15%)
  other arithmetic  31.4 us (10%)
  between operations  14.5 us (5%)
  starting transfers between devices  12.2 us (4%)
    unnamed x36, local copies, waits for them, and re-layouts  47.5 us
    all_gather x2, waiting for transfers between devices, in_one_piece(): lax.all_gather(both, axis, axis=dim, tiled=True)  46.2 us
    all_gather x1, blocking collectives, in_one_piece(): lax.all_gather(both, axis, axis=dim, tiled=True)  22.2 us
    all_gather x1, blocking collectives, body(): lax.all_gather(route_pos, 'ctx', axis=1, tiled=True)  21.4 us
    all_to_all x1, blocking collectives, sent_to_all(): return lax.all_to_all(copies, axis, split_axis=0, concat_axis=0, tiled=True)  20.4 us
    dot_general x1, matrix products, body(): jnp.einsum('hqk,khd->qhd', grad_low, key_heads, preferred_element_type=jn...  16.9 us
    dot_general x1, matrix products, body(): jnp.einsum('hqk,khd->qhd', weights_low, value_heads, preferred_element_ty...  14.8 us
    dot_general x1, matrix products, body(): jnp.einsum('nqhd,khd->nhqk', query_group, own_keys, preferred_element_typ...  14.2 us
  transfers between devices with their start and end apart: 4, of which 3 were waited for; matrix products, arithmetic and copies ran while one was open for 55% of the time, Pallas kernels for 0%

commit v1 on v0

v1 whole, which is shorter than its diff:
```python
import functools

import jax
import jax.numpy as jnp
from jax import lax
from jax.experimental import pallas as pl
from jax.experimental.pallas import tpu as pltpu
from jax.sharding import PartitionSpec as P

HEAD = 128
NEG_FILL = -1e30
LOG2E = 1.4426950408889634
MESH = pl.DeviceIdType.MESH
F32 = jnp.float32
BF16 = jnp.bfloat16
PAIR = 2
NT = (((1,), (1,)), ((), ()))
CH_K, CH_Q, CH_V, CH_D, CH_BIAS, CH_W, CH_GATE, CH_DELTA, CH_TERM, CH_SUM, CH_GQ, CH_GK, CH_GV = range(13)


def kernel(
    n_ctx,
    n_dp,
    total_routed,
    pos_ref,
    w_ref,
    x_hbm,
    q_hbm,
    k_hbm,
    v_hbm,
    d_hbm,
    gq_ref,
    gk_ref,
    gv_ref,
    rg_ref,
    x_v,
    d_v,
    d_send,
    k_all,
    q_all,
    v_all,
    d_all,
    bias_all,
    bias_own,
    w_all,
    w_own,
    gate_all,
    gate_own,
    bias_col,
    kt_all,
    vt_all,
    s_buf,
    e_buf,
    l_buf,
    att_buf,
    ds_t,
    ds_n,
    delta_buf,
    delta_send,
    delta_all,
    dqt,
    gq_send,
    gk_send,
    gv_send,
    term_send,
    term_all,
    sum_send,
    sum_all,
    local_sem,
    send_sem,
    recv_sem,
):
    me = lax.axis_index("ctx")
    me_dp = lax.axis_index("dp")
    rows = q_hbm.shape[0]
    block = PAIR * rows
    blocks = n_ctx // PAIR
    scale = HEAD ** (-0.5)
    chunk = w_ref.shape[1]

    barrier = pltpu.get_barrier_semaphore()
    for o in range(1, n_ctx):
        pl.semaphore_signal(barrier, inc=1, device_id={"ctx": lax.rem(me + o, n_ctx)}, device_id_type=MESH)
    for o in range(1, n_dp):
        pl.semaphore_signal(barrier, inc=1, device_id={"dp": lax.rem(me_dp + o, n_dp)}, device_id_type=MESH)

    def cols(ref, at):
        return ref.at[:, pl.ds(pl.multiple_of(at * HEAD, HEAD), HEAD)]

    local = [
        pltpu.make_async_copy(d_hbm, d_v, local_sem.at[0]),
        pltpu.make_async_copy(x_hbm, x_v, local_sem.at[1]),
        pltpu.make_async_copy(cols(k_hbm, me), k_all.at[me], local_sem.at[2]),
        pltpu.make_async_copy(cols(q_hbm, me), q_all.at[me], local_sem.at[3]),
        pltpu.make_async_copy(cols(v_hbm, me), v_all.at[me], local_sem.at[4]),
    ]
    for copy in local:
        copy.start()

    def remote(src, dst, channel, axis, peer):
        return pltpu.make_async_remote_copy(
            src_ref=src,
            dst_ref=dst,
            send_sem=send_sem.at[channel],
            recv_sem=recv_sem.at[channel],
            device_id={axis: peer},
            device_id_type=MESH,
        )

    def to_peers(source_of, dst, channel, axis, n, mine):
        for o in range(1, n):
            peer = lax.rem(mine + o, n)
            remote(source_of(peer), dst, channel, axis, peer).start()

    def arrived(ref, channel):
        remote(ref, ref, channel, "ctx", lax.rem(me + 1, n_ctx)).wait_recv()

    def sent(ref, channel):
        remote(ref, ref, channel, "ctx", lax.rem(me + 1, n_ctx)).wait_send()

    live = pos_ref[...] >= 0
    bias_row = jnp.broadcast_to(jnp.where(live, 0.0, NEG_FILL).astype(F32), bias_own.shape)
    bias_own[...] = bias_row
    bias_all[me] = bias_row
    w_rows = jnp.broadcast_to(w_ref[...].astype(F32), w_own.shape).astype(BF16)
    w_own[...] = w_rows
    w_all[me_dp] = w_rows
    local[0].wait()
    for h in range(n_ctx):
        d_send[h] = d_v[:, h * HEAD : (h + 1) * HEAD].astype(BF16)
    d_all[me] = d_send[me]

    pl.semaphore_wait(barrier, n_ctx + n_dp - 2)

    to_peers(lambda p: w_own, w_all.at[me_dp], CH_W, "dp", n_dp, me_dp)
    to_peers(lambda p: bias_own, bias_all.at[me], CH_BIAS, "ctx", n_ctx, me)
    to_peers(lambda p: cols(k_hbm, p), k_all.at[me], CH_K, "ctx", n_ctx, me)
    to_peers(lambda p: cols(q_hbm, p), q_all.at[me], CH_Q, "ctx", n_ctx, me)
    to_peers(lambda p: cols(v_hbm, p), v_all.at[me], CH_V, "ctx", n_ctx, me)
    to_peers(lambda p: d_send.at[p], d_all.at[me], CH_D, "ctx", n_ctx, me)

    few = pl.ds(0, n_ctx - 1)
    few_dp = pl.ds(0, n_dp - 1)

    local[1].wait()
    if n_dp > 1:
        arrived(w_all.at[few_dp], CH_W)
    logit = jnp.zeros((16, rows), F32)
    for p in range(n_dp):
        logit += lax.dot_general(w_all[p], x_v[:, p * chunk : (p + 1) * chunk], NT, preferred_element_type=F32)
    gate = jax.nn.sigmoid(logit[0:8])
    gate_live = jnp.where(jnp.broadcast_to(live, gate.shape), gate, 0.0)
    gate_own[...] = gate_live
    gate_all[me] = gate_live

    arrived(bias_all.at[few], CH_BIAS)
    for s in range(n_ctx):
        bias_col[s] = jnp.broadcast_to(bias_all[s][0:1], (HEAD, rows)).T
    to_peers(lambda p: gate_own, gate_all.at[me], CH_GATE, "ctx", n_ctx, me)

    local[2].wait()
    arrived(k_all.at[few], CH_K)

    def pair(ref, at):
        return ref[pl.ds(at * PAIR, PAIR)].reshape(block, HEAD)

    def transposed(src, dst):
        def step(b, carry):
            dst[b] = pair(src, b).T
            return carry

        lax.fori_loop(0, blocks, step, 0)

    transposed(k_all, kt_all)
    local[3].wait()
    arrived(q_all.at[few], CH_Q)

    key_at = lax.broadcasted_iota(jnp.int32, (block, block), 0)
    query_at = lax.broadcasted_iota(jnp.int32, (block, block), 1)
    causal = key_at <= query_at

    def score_block(i, carry):
        q_i = pair(q_all, i)

        def scores(j):
            s = lax.dot_general(pair(k_all, j), q_i, NT, preferred_element_type=F32)
            b = bias_col[pl.ds(j * PAIR, PAIR)].reshape(block, rows)
            return s + jnp.concatenate([b] * PAIR, axis=1)

        def first(j, top):
            s = scores(j)
            s_buf[j] = s
            return jnp.maximum(top, jnp.max(s, axis=0, keepdims=True))

        s_diag = jnp.where(causal, scores(i), NEG_FILL)
        s_buf[i] = s_diag
        top = lax.fori_loop(0, i, first, jnp.max(s_diag, axis=0, keepdims=True))

        def second(j, total):
            e = jnp.exp2((s_buf[j] - top) * (scale * LOG2E))
            e_buf[j, i] = e.astype(BF16)
            return total + jnp.sum(e, axis=0, keepdims=True)

        l_buf[i] = lax.fori_loop(0, i + 1, second, jnp.zeros((1, block), F32))
        return carry

    lax.fori_loop(0, blocks, score_block, 0)

    local[4].wait()
    arrived(v_all.at[few], CH_V)
    transposed(v_all, vt_all)

    def attend_block(i, carry):
        def step(j, acc):
            return acc + jnp.dot(vt_all[j], e_buf[j, i], preferred_element_type=F32)

        att_buf[i] = lax.fori_loop(0, i + 1, step, jnp.zeros((HEAD, block), F32))
        return carry

    lax.fori_loop(0, blocks, attend_block, 0)

    arrived(gate_all.at[few], CH_GATE)
    arrived(d_all.at[few], CH_D)

    def delta_block(i, carry):
        gates = jnp.concatenate([gate_all[i * PAIR + s][0:1] for s in range(PAIR)], axis=1)
        inverse = 1.0 / l_buf[i]
        scaled = (pair(d_all, i).astype(F32).T * (gates * inverse)).astype(BF16)
        ds_t[i] = scaled
        ds_n[i] = scaled.astype(F32).T.astype(BF16)
        delta = jnp.sum(scaled.astype(F32) * att_buf[i], axis=0, keepdims=True)
        delta_buf[i] = delta * inverse
        for s in range(PAIR):
            delta_send[i * PAIR + s] = jnp.broadcast_to(delta[:, s * rows : (s + 1) * rows], (8, rows))
        dqt[i] = jnp.zeros((HEAD, block), F32)
        return carry

    lax.fori_loop(0, blocks, delta_block, 0)
    delta_all[me] = delta_send[me]
    to_peers(lambda p: delta_send.at[p], delta_all.at[me], CH_DELTA, "ctx", n_ctx, me)

    home = me // PAIR

    def send_back(send, out, channel, b):
        for s in range(PAIR):
            peer = b * PAIR + s

            @pl.when(peer != me)
            def _():
                remote(send.at[peer], cols(out, me), channel, "ctx", peer).start()

    def key_block(step, carry):
        j = lax.rem(home + step, blocks)
        v_j = pair(v_all, j)

        def inner(i, acc):
            dk, dv = acc
            e = e_buf[j, i]
            dw = jnp.dot(v_j, ds_t[i], preferred_element_type=F32)
            g = (e.astype(F32) * (dw - delta_buf[i])).astype(BF16)
            dk += jnp.dot(g, pair(q_all, i), preferred_element_type=F32)
            dv += jnp.dot(e, ds_n[i], preferred_element_type=F32)
            dqt[i] += jnp.dot(kt_all[j], g, preferred_element_type=F32)
            return dk, dv

        zero = jnp.zeros((block, HEAD), F32)
        dk, dv = lax.fori_loop(j, blocks, inner, (zero, zero))
        gk_send[pl.ds(j * PAIR, PAIR)] = (dk * scale).astype(BF16).reshape(PAIR, rows, HEAD)
        gv_send[pl.ds(j * PAIR, PAIR)] = dv.astype(BF16).reshape(PAIR, rows, HEAD)

        @pl.when(step > 0)
        def _():
            before = lax.rem(home + step + blocks - 1, blocks)
            send_back(gk_send, gk_ref, CH_GK, before)
            send_back(gv_send, gv_ref, CH_GV, before)

        return carry

    lax.fori_loop(0, blocks, key_block, 0)
    last = lax.rem(home + blocks - 1, blocks)
    send_back(gk_send, gk_ref, CH_GK, last)
    send_back(gv_send, gv_ref, CH_GV, last)

    def query_out(b, carry):
        gq_send[pl.ds(b * PAIR, PAIR)] = (dqt[b] * scale).T.astype(BF16).reshape(PAIR, rows, HEAD)
        return carry

    lax.fori_loop(0, blocks, query_out, 0)
    to_peers(lambda p: gq_send.at[p], cols(gq_ref, me), CH_GQ, "ctx", n_ctx, me)
    own = [
        pltpu.make_async_copy(gq_send.at[me], cols(gq_ref, me), local_sem.at[5]),
        pltpu.make_async_copy(gk_send.at[me], cols(gk_ref, me), local_sem.at[6]),
        pltpu.make_async_copy(gv_send.at[me], cols(gv_ref, me), local_sem.at[7]),
    ]
    for copy in own:
        copy.start()

    arrived(delta_all.at[few], CH_DELTA)
    row_sum = delta_all[0]
    for h in range(1, n_ctx):
        row_sum += delta_all[h]
    grad_logit = row_sum * (1.0 - gate)
    high = grad_logit.astype(BF16)
    rest = grad_logit - high.astype(F32)
    middle = rest.astype(BF16)
    low = (rest - middle.astype(F32)).astype(BF16)
    which = lax.broadcasted_iota(jnp.int32, (8, rows), 0)
    split = jnp.where(which == 0, high.astype(F32), jnp.where(which == 1, middle.astype(F32), low.astype(F32)))
    split = jnp.where(which < 3, split, 0.0).astype(BF16)
    for p in range(n_dp):
        term_send[p] = jnp.dot(split, x_v[:, p * chunk : (p + 1) * chunk], preferred_element_type=F32)
    term_all[me_dp] = term_send[me_dp]
    to_peers(lambda p: term_send.at[p], term_all.at[me_dp], CH_TERM, "dp", n_dp, me_dp)
    if n_dp > 1:
        arrived(term_all.at[few_dp], CH_TERM)
    term_sum = term_all[0]
    for p in range(1, n_dp):
        term_sum += term_all[p]
    term_sum = jnp.broadcast_to(jnp.sum(term_sum, axis=0, keepdims=True), sum_send.shape)
    sum_send[...] = term_sum
    sum_all[me] = term_sum
    to_peers(lambda p: sum_send, sum_all.at[me], CH_SUM, "ctx", n_ctx, me)
    arrived(sum_all.at[few], CH_SUM)
    everything = sum_all[0]
    for c in range(1, n_ctx):
        everything += sum_all[c]
    rg_ref[...] = everything * (1.0 / total_routed)

    most = pl.ds(0, (n_ctx - 1) * HEAD)
    arrived(gk_ref.at[:, most], CH_GK)
    arrived(gv_ref.at[:, most], CH_GV)
    arrived(gq_ref.at[:, most], CH_GQ)
    for copy in own:
        copy.wait()
    for ref, channel in (
        (k_all, CH_K),
        (q_all, CH_Q),
        (v_all, CH_V),
        (d_all, CH_D),
        (bias_all, CH_BIAS),
        (gate_all, CH_GATE),
        (delta_all, CH_DELTA),
        (sum_all, CH_SUM),
        (gq_send, CH_GQ),
        (gk_send, CH_GK),
        (gv_send, CH_GV),
    ):
        sent(ref.at[few], channel)
    if n_dp > 1:
        sent(w_all.at[few_dp], CH_W)
        sent(term_all.at[few_dp], CH_TERM)


def body(route_pos, x_routed, w_router, queries, keys, values, d_gated):
    n_ctx = lax.axis_size("ctx")
    n_dp = lax.axis_size("dp")
    rows, width = queries.shape[1:]
    blocks = n_ctx // PAIR
    block = PAIR * rows
    total_routed = float(n_dp * n_ctx * rows // 2)
    chunk = w_router.shape[0]
    vmem = pl.BlockSpec(memory_space=pltpu.VMEM)
    anywhere = pl.BlockSpec(memory_space=pl.ANY)
    heads = pltpu.VMEM((n_ctx, rows, HEAD), BF16)
    small = pltpu.VMEM((n_ctx, 8, rows), F32)
    small_own = pltpu.VMEM((8, rows), F32)
    out = jax.ShapeDtypeStruct((rows, width), BF16)
    gq, gk, gv, rg = pl.pallas_call(
        functools.partial(kernel, n_ctx, n_dp, total_routed),
        out_shape=(out, out, out, jax.ShapeDtypeStruct((8, chunk), F32)),
        in_specs=[vmem, vmem] + [anywhere] * 5,
        out_specs=(anywhere, anywhere, anywhere, vmem),
        scratch_shapes=[
            pltpu.VMEM(x_routed.shape[1:], BF16),
            pltpu.VMEM((rows, width), F32),
            heads,
            heads,
            heads,
            heads,
            heads,
            small,
            small_own,
            pltpu.VMEM((n_dp, 16, chunk), BF16),
            pltpu.VMEM((16, chunk), BF16),
            small,
            small_own,
            pltpu.VMEM((n_ctx, rows, rows), F32),
            pltpu.VMEM((blocks, HEAD, block), BF16),
            pltpu.VMEM((blocks, HEAD, block), BF16),
            pltpu.VMEM((blocks, block, block), F32),
            pltpu.VMEM((blocks, blocks, block, block), BF16),
            pltpu.VMEM((blocks, 1, block), F32),
            pltpu.VMEM((blocks, HEAD, block), F32),
            pltpu.VMEM((blocks, HEAD, block), BF16),
            pltpu.VMEM((blocks, block, HEAD), BF16),
            pltpu.VMEM((blocks, 1, block), F32),
            small,
            small,
            pltpu.VMEM((blocks, HEAD, block), F32),
            heads,
            heads,
            heads,
            pltpu.VMEM((n_dp, 8, chunk), F32),
            pltpu.VMEM((n_dp, 8, chunk), F32),
            pltpu.VMEM((8, chunk), F32),
            pltpu.VMEM((n_ctx, 8, chunk), F32),
            pltpu.SemaphoreType.DMA((8,)),
            pltpu.SemaphoreType.DMA((13,)),
            pltpu.SemaphoreType.DMA((13,)),
        ],
        compiler_params=pltpu.CompilerParams(collective_id=0, has_side_effects=True, vmem_limit_bytes=56 * 1024 * 1024),
        name="routed_backward",
    )(route_pos, w_router[None], x_routed[0], queries[0], keys[0], values[0], d_gated[0])
    return (gq.astype(F32)[None], gk.astype(F32)[None], gv.astype(F32)[None], rg[0])


def solution(mesh):
    placed = (
        P("dp", "ctx"),
        P("dp", "ctx", None),
        P("dp"),
        P("dp", "ctx", None),
        P("dp", "ctx", None),
        P("dp", "ctx", None),
        P("dp", "ctx", None),
    )
    return jax.shard_map(
        body,
        mesh=mesh,
        in_specs=placed,
        out_specs=(P("dp", "ctx", None), P("dp", "ctx", None), P("dp", "ctx", None), P("dp")),
        check_vma=False,
    )
```

time: 322 us -> 91 us (0.28); the launches traced: 318 us -> 90.8 us
  matrix products: 87 us -> 0 us
  Pallas kernels: 0 us -> 83.8 us
  blocking collectives: 64 us -> 0 us
  local copies, waits for them, and re-layouts: 61.7 us -> 2.48 us
  waiting for transfers between devices: 47 us -> 0 us
  other arithmetic: 31.4 us -> 3.89 us
  between operations: 14.5 us -> 0.65 us
  starting transfers between devices: 12.2 us -> 0 us
    dot_general x9 -> x0, matrix products: 87 us -> none  [the longest x1 16.9 us: body(): jnp.einsum('hqk,khd->qhd', grad_low, key_heads, preferred_element_type=jn...]
    pallas_call x0 -> x1, Pallas kernels: none -> 83.8 us  [body(): pl.pallas_call(functools.partial(kernel, n_ctx, n_dp, total_routed), out_...]
    unnamed x36 -> x2, local copies, waits for them, and re-layouts: 47.5 us -> 0.01 us
    all_gather x2 -> x0, waiting for transfers between devices: 46.2 us -> none  [in_one_piece(): lax.all_gather(both, axis, axis=dim, tiled=True)]
    all_gather x2 -> x0, blocking collectives: 43.6 us -> none  [the longest x1 22.2 us: in_one_piece(): lax.all_gather(both, axis, axis=dim, tiled=True)]
    reduce_sum x5 -> x0, other arithmetic: 20.9 us -> none  [the longest x1 9.45 us: body(): row_total = jnp.sum(exponent, axis=-1, keepdims=True)]
    all_to_all x1 -> x0, blocking collectives: 20.4 us -> none  [sent_to_all(): return lax.all_to_all(copies, axis, split_axis=0, concat_axis=0, tiled=True)]
    all_to_all x2 -> x0, starting transfers between devices: 12.1 us -> none  [the longest x1 8.35 us: summed_on_arrival(): lax.all_to_all(in_blocks(array, dim, devices), axis, 0, 0, tiled=True)]
  transfers between devices with their start and end apart: 4 -> 0, of which waited for: 3 -> 0; matrix products, arithmetic and copies ran while one was open for 55% -> 0% of each run, Pallas kernels for 0% -> 0%
where the time goes in v1:
time: 91 us; the launch traced here: 90.8 us
  Pallas kernels  83.8 us (92%)
  other arithmetic  3.89 us (4%)
  local copies, waits for them, and re-layouts  2.48 us (3%)
    pallas_call x1, Pallas kernels, body(): pl.pallas_call(functools.partial(kernel, n_ctx, n_dp, total_routed), out_...  83.8 us
    broadcast_in_dim x1, other arithmetic, body(): gv.astype(F32)[None]  2.82 us

profile of v1, /device:TPU:1, one launch (start us, length us, event | category | flops | bytes accessed | tf_op | source)
XLA Modules:
  0.0 90.8 jit_solution(18341366107350449885)
XLA Ops:
  0.6 1.2 %broadcast_in_dim.21.w_ref = bf16[1,256]{1,0:T(2,128)(2,1)} reshape(bf16[256]{0:T(256)(128)(2,1)} %param.9) | data formatting | bytes 1024 | tf_op jit(solution)/shard_map/broadcast_in_dim | solution.py:413
  1.9 83.8 %routed_backward.1 = (bf16[128,2048]{1,0:T(8,128)(2,1)}, bf16[128,2048]{1,0:T(8,128)(2,1)}, bf16[128,2048]{1,0:T(8,128)(2,1)}, f32[8,256]{1,0:T(8,128)}) custom-call(s32[1,128]{1,0:T(1,128)} %pos_ref.1, bf16[1,256]{1,0:T(2,128)(2,1)} %broadcast_in_dim.21.w_ref, bf16[128,4096]{1,0:T(8,128)(2,1)} %bitcast.15, bf16[128,2048]{1,0:T(8,128)(2,1)} %bitcast.17, ...), custom_call_target="tpu_custom_call" | custom-call | tf_op jit(solution)/shard_map/routed_backward/pallas_call | solution.py:368
  85.6 0.0 copy-start
  85.6 2.8 %bitcast_convert_fusion = (f32[1,128,2048]{2,1,0:T(8,128)}, f32[1,128,2048]{2,1,0:T(8,128)}) fusion(bf16[128,2048]{1,0:T(8,128)(2,1)} %get-tuple-element.10, bf16[128,2048]{1,0:T(8,128)(2,1)} %get-tuple-element.9), kind=kLoop, calls=%fused_computation | loop fusion | flops 524288 | bytes 3145728 | tf_op jit(solution)/shard_map/broadcast_in_dim | solution.py:414
  88.5 0.0 copy-done
  88.5 1.1 %bitcast_convert_fusion.2 = f32[1,128,2048]{2,1,0:T(8,128)} fusion(bf16[128,2048]{1,0:T(8,128)(2,1)S(1)} %copy-done), kind=kLoop, calls=%fused_computation.2 | loop fusion | flops 262144 | bytes 1572864 | tf_op jit(solution)/shard_map/broadcast_in_dim | solution.py:414
  89.5 1.3 %slice.3 = f32[1,256]{1,0:T(1,128)} slice(f32[8,256]{1,0:T(8,128)} %get-tuple-element.11), slice={[0:1], [0:256]} | slice | bytes 2048 | tf_op jit(solution)/shard_map/slice | solution.py:414
Async XLA Ops:
  85.6 2.8 %copy-start = (bf16[128,2048]{1,0:T(8,128)(2,1)S(1)}, bf16[128,2048]{1,0:T(8,128)(2,1)}, u32[]{:S(2)}) copy-start(bf16[128,2048]{1,0:T(8,128)(2,1)} %get-tuple-element.8) | copy-start | bytes 1572868

commit v2 on v1

v2 whole, which is shorter than its diff:
```python
import functools

import jax
import jax.numpy as jnp
from jax import lax
from jax.experimental import pallas as pl
from jax.experimental.pallas import tpu as pltpu
from jax.sharding import PartitionSpec as P

HEAD = 128
NEG_FILL = -1e30
LOG2E = 1.4426950408889634
MESH = pl.DeviceIdType.MESH
F32 = jnp.float32
BF16 = jnp.bfloat16
BLOCK = 256
NT = (((1,), (1,)), ((), ()))
CH_K, CH_Q, CH_V, CH_D, CH_LIVE, CH_W_Z, CH_W_Y, CH_DELTA, CH_TERM_Y, CH_TERM_Z, CH_SUM, CH_GQ, CH_GK, CH_GV = range(14)
CHANNELS = 14


def dot(a, b):
    return jnp.dot(a, b, preferred_element_type=F32)


def dot_nt(a, b):
    return lax.dot_general(a, b, NT, preferred_element_type=F32)


def three_rows(row):
    high = row.astype(BF16).astype(F32)
    middle = (row - high).astype(BF16).astype(F32)
    low = row - high - middle
    which = lax.broadcasted_iota(jnp.int32, row.shape, 0)
    split = jnp.where(which == 0, high, jnp.where(which == 1, middle, low))
    return jnp.where(which < 3, split, 0.0).astype(BF16)


def kernel(
    n_ctx,
    n_y,
    n_z,
    pos_ref,
    w_ref,
    x_hbm,
    q_hbm,
    k_hbm,
    v_hbm,
    d_hbm,
    gq_ref,
    gk_ref,
    gv_ref,
    rg_ref,
    x_v,
    d_v,
    d_send,
    kq_all,
    v_all,
    d_all,
    live_all,
    live_own,
    w_all,
    rank_row,
    pick,
    place,
    kq_c,
    kt_c,
    v_c,
    d_c,
    p_buf,
    ds_buf,
    gkq_c,
    gv_c,
    delta_send,
    delta_all,
    gq_send,
    gk_send,
    gv_send,
    term_send,
    term_y,
    term_half,
    term_z,
    sum_send,
    sum_all,
    local_sem,
    send_sem,
    recv_sem,
):
    me = lax.axis_index("ctx")
    me_dp = lax.axis_index("dp")
    n_dp = n_y * n_z
    me_y, me_z = me_dp // n_z, lax.rem(me_dp, n_z)
    rows = q_hbm.shape[0]
    slots = n_ctx * rows
    routed = slots // 2
    blocks = routed // BLOCK
    per_block = BLOCK // rows
    scale = HEAD ** (-0.5)
    chunk = w_all.shape[2]
    total_routed = float(n_dp * routed)

    def z_peer(o):
        return me_y * n_z + lax.rem(me_z + o, n_z)

    def y_peer(o):
        return lax.rem(me_y + o, n_y) * n_z + me_z

    barrier = pltpu.get_barrier_semaphore()
    for o in range(1, n_z):
        pl.semaphore_signal(barrier, inc=1, device_id={"dp": z_peer(o)}, device_id_type=MESH)
    for o in range(1, n_y):
        pl.semaphore_signal(barrier, inc=1, device_id={"dp": y_peer(o)}, device_id_type=MESH)
    for o in range(1, n_ctx):
        pl.semaphore_signal(barrier, inc=1, device_id={"ctx": lax.rem(me + o, n_ctx)}, device_id_type=MESH)

    def cols(ref, at):
        return ref.at[:, pl.ds(pl.multiple_of(at * HEAD, HEAD), HEAD)]

    local = [
        pltpu.make_async_copy(d_hbm, d_v, local_sem.at[0]),
        pltpu.make_async_copy(x_hbm, x_v, local_sem.at[1]),
        pltpu.make_async_copy(cols(k_hbm, me), kq_all.at[me, :, pl.ds(0, HEAD)], local_sem.at[2]),
        pltpu.make_async_copy(cols(q_hbm, me), kq_all.at[me, :, pl.ds(HEAD, HEAD)], local_sem.at[3]),
        pltpu.make_async_copy(cols(v_hbm, me), v_all.at[me], local_sem.at[4]),
    ]
    for copy in local:
        copy.start()

    def remote(src, dst, channel, axis, peer):
        return pltpu.make_async_remote_copy(
            src_ref=src,
            dst_ref=dst,
            send_sem=send_sem.at[channel],
            recv_sem=recv_sem.at[channel],
            device_id={axis: peer},
            device_id_type=MESH,
        )

    def to_peers(source_of, dst, channel, axis, n, mine):
        for o in range(1, n):
            peer = lax.rem(mine + o, n)
            remote(source_of(peer), dst, channel, axis, peer).start()

    def arrived(ref, channel):
        remote(ref, ref, channel, "ctx", lax.rem(me + 1, n_ctx)).wait_recv()

    def sent(ref, channel):
        remote(ref, ref, channel, "ctx", lax.rem(me + 1, n_ctx)).wait_send()

    few = pl.ds(0, n_ctx - 1)

    live_row = jnp.where(jnp.broadcast_to(pos_ref[...], (8, rows)) >= 0, 1.0, 0.0).astype(F32)
    live_own[...] = live_row[0:1]
    live_all[me] = live_row[0:1]
    w_all[me_dp] = w_ref[...].reshape(1, chunk)

    pl.semaphore_wait(barrier, n_ctx + n_y + n_z - 3)

    for o in range(1, n_z):
        remote(w_all.at[me_dp], w_all.at[me_dp], CH_W_Z, "dp", z_peer(o)).start()
    to_peers(lambda p: live_own, live_all.at[me], CH_LIVE, "ctx", n_ctx, me)
    to_peers(lambda p: cols(k_hbm, p), kq_all.at[me, :, pl.ds(0, HEAD)], CH_K, "ctx", n_ctx, me)
    to_peers(lambda p: cols(q_hbm, p), kq_all.at[me, :, pl.ds(HEAD, HEAD)], CH_Q, "ctx", n_ctx, me)
    to_peers(lambda p: cols(v_hbm, p), v_all.at[me], CH_V, "ctx", n_ctx, me)

    local[1].wait()
    if n_z > 1:
        arrived(w_all.at[pl.ds(0, n_z - 1)], CH_W_Z)
    own_y = pl.ds(me_y * n_z, n_z)
    for o in range(1, n_y):
        remote(w_all.at[own_y], w_all.at[own_y], CH_W_Y, "dp", y_peer(o)).start()
    if n_y > 1:
        arrived(w_all.at[pl.ds(0, (n_y - 1) * n_z)], CH_W_Y)
    logit = jnp.zeros((rows, rows), F32)
    for p in range(n_dp):
        w_p = jnp.broadcast_to(w_all[p].astype(F32), (rows, chunk)).astype(BF16)
        logit += dot_nt(x_v[:, p * chunk : (p + 1) * chunk], w_p)
    gate = jax.nn.sigmoid(logit)
    gate_row = gate.T[0:8]
    factor = gate * jnp.broadcast_to(live_row[0:1], (rows, rows)).T
    local[0].wait()
    for h in range(n_ctx):
        d_send[h] = (d_v[:, h * HEAD : (h + 1) * HEAD] * factor).astype(BF16)
    d_all[me] = d_send[me]

    arrived(live_all.at[few], CH_LIVE)
    lane = lax.broadcasted_iota(jnp.int32, (8, rows), 1).astype(F32)
    before = jnp.zeros((8, rows), F32)
    for s in range(n_ctx):
        live_s = jnp.broadcast_to(live_all[s], (8, rows))
        rank_row[s] = jnp.where(live_s > 0.0, before + lane, -1.0)
        before = before + jnp.sum(live_s, axis=1, keepdims=True)

    to_peers(lambda p: d_send.at[p], d_all.at[me], CH_D, "ctx", n_ctx, me)

    token_row = lax.broadcasted_iota(jnp.int32, (BLOCK, rows), 0).astype(F32)
    token_lane = lax.broadcasted_iota(jnp.int32, (rows, routed), 1).astype(F32)

    def slots_of(b):
        first = b * per_block
        return first, min(n_ctx, first + (routed + BLOCK) // rows)

    for b in range(blocks):
        first, last = slots_of(b)
        for s in range(first, last):
            rank = jnp.broadcast_to(rank_row[s][0:1], (BLOCK, rows))
            hit = jnp.where(token_row + float(b * BLOCK) == rank, 1.0, 0.0)
            pick[b, :, (s - first) * rows : (s - first + 1) * rows] = hit.astype(BF16)

    def place_step(s, carry):
        rank = jnp.broadcast_to(rank_row[s][0:1], (rows, rows)).T
        rank = jnp.concatenate([rank] * (routed // rows), axis=1)
        place[s] = jnp.where(token_lane == rank, 1.0, 0.0).astype(BF16)
        return carry

    lax.fori_loop(0, n_ctx, place_step, 0)

    def packed(all_ref, b):
        first, last = slots_of(b)
        source = all_ref[first:last]
        width = (last - first) * rows
        return dot(pick[b, :, 0:width], source.reshape(width, source.shape[2])).astype(BF16)

    def span(b, e=1):
        return slice(b * BLOCK, (b + e) * BLOCK)

    local[2].wait()
    local[3].wait()
    arrived(v_all.at[few], CH_K)
    arrived(v_all.at[few], CH_Q)
    for b in range(blocks):
        kq_c[span(b)] = packed(kq_all, b)
    for b in range(blocks):
        kt_c[:, span(b)] = kq_c[span(b), 0:HEAD].astype(F32).T.astype(BF16)

    key_at = lax.broadcasted_iota(jnp.int32, (BLOCK, BLOCK), 0)
    query_at = lax.broadcasted_iota(jnp.int32, (BLOCK, BLOCK), 1)
    causal = key_at <= query_at
    for i in range(blocks):
        q_i = kq_c[span(i), HEAD : 2 * HEAD]
        parts = [dot_nt(kq_c[span(j), 0:HEAD], q_i) for j in range(i + 1)]
        parts[i] = jnp.where(causal, parts[i], NEG_FILL)
        top = functools.reduce(jnp.maximum, [jnp.max(s, axis=0, keepdims=True) for s in parts])
        parts = [jnp.exp2((s - top) * (scale * LOG2E)) for s in parts]
        total = functools.reduce(jnp.add, [jnp.sum(e, axis=0, keepdims=True) for e in parts])
        inverse = 1.0 / total
        for j in range(i + 1):
            p_buf[span(j), span(i)] = (parts[j] * inverse).astype(BF16)

    local[4].wait()
    arrived(v_all.at[few], CH_V)
    for b in range(blocks):
        v_c[span(b)] = packed(v_all, b)

    arrived(d_all.at[few], CH_D)
    for b in range(blocks):
        d_c[span(b)] = packed(d_all, b)

    for j in range(blocks):
        rest = slice(j * BLOCK, routed)
        gv_c[span(j)] = dot(p_buf[span(j), rest], d_c[rest]).astype(BF16)

    def unpacked(m, source, low, high):
        begin = max(0, (m + 1) * BLOCK - BLOCK - routed)
        end = min(routed, (m + 1) * BLOCK)
        hits = place[m * per_block : (m + 1) * per_block].reshape(BLOCK, routed)
        return dot(hits[:, begin:end], source[begin:end, low:high])

    pairs = n_ctx // per_block
    for m in range(pairs):
        both = unpacked(m, gv_c, 0, HEAD).astype(BF16).reshape(per_block, rows, HEAD)
        gv_send[m * per_block : (m + 1) * per_block] = both

    delta_slots = [jnp.zeros((8, rows), F32) for _ in range(n_ctx)]
    for i in range(blocks):
        d_i = d_c[span(i)]
        terms, weights = [], []
        for j in range(i + 1):
            p_ji = p_buf[span(j), span(i)].astype(F32)
            weights.append(p_ji)
            terms.append(p_ji * dot_nt(v_c[span(j)], d_i))
        delta = functools.reduce(jnp.add, [jnp.sum(t, axis=0, keepdims=True) for t in terms])
        for j in range(i + 1):
            ds_buf[span(j), span(i)] = (terms[j] - weights[j] * delta).astype(BF16)
        first, last = slots_of(i)
        width = (last - first) * rows
        moved = dot(three_rows(jnp.broadcast_to(delta, (8, BLOCK))), pick[i, :, 0:width])
        for s in range(first, last):
            delta_slots[s] = delta_slots[s] + moved[:, (s - first) * rows : (s - first + 1) * rows]
    for s in range(n_ctx):
        delta_send[s] = jnp.sum(delta_slots[s], axis=0, keepdims=True)
    delta_all[me] = delta_send[me]

    to_peers(lambda p: gv_send.at[p], cols(gv_ref, me), CH_GV, "ctx", n_ctx, me)
    to_peers(lambda p: delta_send.at[p], delta_all.at[me], CH_DELTA, "ctx", n_ctx, me)

    for j in range(blocks):
        rest = slice(j * BLOCK, routed)
        gkq_c[span(j), 0:HEAD] = (dot(ds_buf[span(j), rest], kq_c[rest, HEAD : 2 * HEAD]) * scale).astype(BF16)
    for i in range(blocks):
        upto = slice(0, (i + 1) * BLOCK)
        gkq_c[span(i), HEAD : 2 * HEAD] = (dot(kt_c[:, upto], ds_buf[upto, span(i)]) * scale).T.astype(BF16)
    for m in range(pairs):
        both = unpacked(m, gkq_c, 0, 2 * HEAD).astype(BF16)
        gk_send[m * per_block : (m + 1) * per_block] = both[:, 0:HEAD].reshape(per_block, rows, HEAD)
        gq_send[m * per_block : (m + 1) * per_block] = both[:, HEAD : 2 * HEAD].reshape(per_block, rows, HEAD)

    arrived(delta_all.at[few], CH_DELTA)
    row_sum = delta_all[0]
    for h in range(1, n_ctx):
        row_sum += delta_all[h]
    row_sum = jnp.broadcast_to(row_sum, (8, rows))
    split = three_rows(row_sum * (1.0 - gate_row))
    for p in range(n_dp):
        term_send[p] = jnp.sum(dot(split, x_v[:, p * chunk : (p + 1) * chunk]), axis=0, keepdims=True)
    term_y[me_y] = term_send[own_y]
    for o in range(1, n_y):
        group = pl.ds(lax.rem(me_y + o, n_y) * n_z, n_z)
        remote(term_send.at[group], term_y.at[me_y], CH_TERM_Y, "dp", y_peer(o)).start()
    to_peers(lambda p: gk_send.at[p], cols(gk_ref, me), CH_GK, "ctx", n_ctx, me)
    own = [
        pltpu.make_async_copy(gq_send.at[me], cols(gq_ref, me), local_sem.at[5]),
        pltpu.make_async_copy(gk_send.at[me], cols(gk_ref, me), local_sem.at[6]),
        pltpu.make_async_copy(gv_send.at[me], cols(gv_ref, me), local_sem.at[7]),
    ]
    for copy in own:
        copy.start()
    if n_y > 1:
        arrived(term_y.at[pl.ds(0, n_y - 1)], CH_TERM_Y)
    half = term_y[0]
    for p in range(1, n_y):
        half += term_y[p]
    term_half[...] = half
    term_z[me_z] = term_half[me_z]
    for o in range(1, n_z):
        remote(term_half.at[lax.rem(me_z + o, n_z)], term_z.at[me_z], CH_TERM_Z, "dp", z_peer(o)).start()
    if n_z > 1:
        arrived(term_z.at[pl.ds(0, n_z - 1)], CH_TERM_Z)
    term_sum = term_z[0]
    for p in range(1, n_z):
        term_sum += term_z[p]
    sum_send[...] = term_sum
    sum_all[me] = term_sum
    to_peers(lambda p: sum_send, sum_all.at[me], CH_SUM, "ctx", n_ctx, me)
    to_peers(lambda p: gq_send.at[p], cols(gq_ref, me), CH_GQ, "ctx", n_ctx, me)
    arrived(sum_all.at[few], CH_SUM)
    everything = sum_all[0]
    for c in range(1, n_ctx):
        everything += sum_all[c]
    rg_ref[...] = everything * (1.0 / total_routed)

    most = pl.ds(0, (n_ctx - 1) * HEAD)
    arrived(gv_ref.at[:, most], CH_GV)
    arrived(gk_ref.at[:, most], CH_GK)
    arrived(gq_ref.at[:, most], CH_GQ)
    for copy in own:
        copy.wait()
    for ref, channel in (
        (v_all, CH_K),
        (v_all, CH_Q),
        (v_all, CH_V),
        (d_all, CH_D),
        (live_all, CH_LIVE),
        (delta_all, CH_DELTA),
        (sum_all, CH_SUM),
        (gq_send, CH_GQ),
        (gk_send, CH_GK),
        (gv_send, CH_GV),
    ):
        sent(ref.at[few], channel)
    if n_z > 1:
        sent(w_all.at[pl.ds(0, n_z - 1)], CH_W_Z)
        sent(term_z.at[pl.ds(0, n_z - 1)], CH_TERM_Z)
    if n_y > 1:
        sent(w_all.at[pl.ds(0, (n_y - 1) * n_z)], CH_W_Y)
        sent(term_y.at[pl.ds(0, n_y - 1)], CH_TERM_Y)


def widen(gq_ref, gk_ref, gv_ref, rg_ref, q_out, k_out, v_out, r_out):
    q_out[...] = gq_ref[...].astype(F32)
    k_out[...] = gk_ref[...].astype(F32)
    v_out[...] = gv_ref[...].astype(F32)
    r_out[...] = rg_ref[0]


def body(route_pos, x_routed, w_router, queries, keys, values, d_gated):
    n_ctx = lax.axis_size("ctx")
    n_dp = lax.axis_size("dp")
    n_z = 4 if n_dp >= 16 else min(2, n_dp)
    n_y = n_dp // n_z
    rows, width = queries.shape[1:]
    routed = n_ctx * rows // 2
    blocks = routed // BLOCK
    chunk = w_router.shape[0]
    vmem = pl.BlockSpec(memory_space=pltpu.VMEM)
    hbm = pl.BlockSpec(memory_space=pltpu.HBM)
    heads = pltpu.VMEM((n_ctx, rows, HEAD), BF16)
    small = pltpu.VMEM((n_ctx, 1, rows), F32)
    compact = pltpu.VMEM((routed, HEAD), BF16)
    square = pltpu.VMEM((routed, routed), BF16)
    out = jax.ShapeDtypeStruct((rows, width), BF16)
    gq, gk, gv, rg = pl.pallas_call(
        functools.partial(kernel, n_ctx, n_y, n_z),
        out_shape=(out, out, out, jax.ShapeDtypeStruct((1, chunk), F32)),
        in_specs=[vmem, vmem] + [hbm] * 5,
        out_specs=(hbm, hbm, hbm, vmem),
        scratch_shapes=[
            pltpu.VMEM(x_routed.shape[1:], BF16),
            pltpu.VMEM((rows, width), F32),
            heads,
            pltpu.VMEM((n_ctx, rows, 2 * HEAD), BF16),
            heads,
            heads,
            small,
            pltpu.VMEM((1, rows), F32),
            pltpu.VMEM((n_dp, 1, chunk), BF16),
            pltpu.VMEM((n_ctx, 8, rows), F32),
            pltpu.VMEM((blocks, BLOCK, routed + BLOCK), BF16),
            pltpu.VMEM((n_ctx, rows, routed), BF16),
            pltpu.VMEM((routed, 2 * HEAD), BF16),
            pltpu.VMEM((HEAD, routed), BF16),
            compact,
            compact,
            square,
            square,
            pltpu.VMEM((routed, 2 * HEAD), BF16),
            compact,
            small,
            small,
            heads,
            heads,
            heads,
            pltpu.VMEM((n_dp, 1, chunk), F32),
            pltpu.VMEM((n_y, n_z, 1, chunk), F32),
            pltpu.VMEM((n_z, 1, chunk), F32),
            pltpu.VMEM((n_z, 1, chunk), F32),
            pltpu.VMEM((1, chunk), F32),
            pltpu.VMEM((n_ctx, 1, chunk), F32),
            pltpu.SemaphoreType.DMA((8,)),
            pltpu.SemaphoreType.DMA((CHANNELS,)),
            pltpu.SemaphoreType.DMA((CHANNELS,)),
        ],
        compiler_params=pltpu.CompilerParams(collective_id=0, has_side_effects=True, vmem_limit_bytes=60 * 1024 * 1024),
        name="routed_backward",
    )(route_pos, w_router, x_routed[0], queries[0], keys[0], values[0], d_gated[0])
    steps = 4
    tile = pl.BlockSpec((rows // steps, width), lambda i: (i, 0))
    wide = jax.ShapeDtypeStruct((rows, width), F32)
    gq, gk, gv, rg = pl.pallas_call(
        widen,
        grid=(steps,),
        out_shape=(wide, wide, wide, jax.ShapeDtypeStruct((chunk,), F32)),
        in_specs=[tile, tile, tile, pl.BlockSpec((1, chunk), lambda i: (0, 0))],
        out_specs=(tile, tile, tile, pl.BlockSpec((chunk,), lambda i: (0,))),
        name="widen",
    )(gq, gk, gv, rg)
    return (gq[None], gk[None], gv[None], rg)


def solution(mesh):
    placed = (
        P("dp", "ctx"),
        P("dp", "ctx", None),
        P("dp"),
        P("dp", "ctx", None),
        P("dp", "ctx", None),
        P("dp", "ctx", None),
        P("dp", "ctx", None),
    )
    return jax.shard_map(
        body,
        mesh=mesh,
        in_specs=placed,
        out_specs=(P("dp", "ctx", None), P("dp", "ctx", None), P("dp", "ctx", None), P("dp")),
        check_vma=False,
    )
```

time: 91 us -> 69.9 us (0.77)
  Pallas kernels: 83.8 us -> 69.1 us
  other arithmetic: 3.89 us -> 0 us
  local copies, waits for them, and re-layouts: 2.48 us -> 0 us
    pallas_call x1 -> x2, Pallas kernels: 83.8 us -> 69.1 us  [the longest x1 65.2 us: body(): pl.pallas_call(functools.partial(kernel, n_ctx, n_y, n_z), out_shape=(out...]
    broadcast_in_dim x2 -> x0, other arithmetic: 3.89 us -> none  [the longest x1 2.82 us: body(): gv.astype(F32)[None]]
    slice x1 -> x0, local copies, waits for them, and re-layouts: 1.26 us -> none  [body(): rg[0]]
    broadcast_in_dim x1 -> x0, local copies, waits for them, and re-layouts: 1.22 us -> none  [body(): w_router[None]]
where the time goes in v2:
time: 69.9 us; the launch traced here: 69.8 us
  Pallas kernels  69.1 us (99%)
    pallas_call x1, Pallas kernels, body(): pl.pallas_call(functools.partial(kernel, n_ctx, n_y, n_z), out_shape=(out...  65.2 us
    pallas_call x1, Pallas kernels, body(): pl.pallas_call(widen, grid=(steps,), out_shape=(wide, wide, wide, jax.Sha...  3.91 us

profile of v2, /device:TPU:1, one launch (start us, length us, event | category | flops | bytes accessed | tf_op | source)
XLA Modules:
  0.0 69.8 jit_solution(7176484942060599421)
XLA Ops:
  0.6 65.2 %routed_backward.1 = (bf16[128,2048]{1,0:T(8,128)(2,1)}, bf16[128,2048]{1,0:T(8,128)(2,1)}, bf16[128,2048]{1,0:T(8,128)(2,1)}, f32[1,256]{1,0:T(1,128)}) custom-call(s32[1,128]{1,0:T(1,128)} %pos_ref.1, bf16[256]{0:T(256)(128)(2,1)} %w_ref.1, bf16[128,4096]{1,0:T(8,128)(2,1)} %bitcast.8, bf16[128,2048]{1,0:T(8,128)(2,1)} %bitcast.10, ...), custom_call_target="tpu_custom_call" | custom-call | tf_op jit(solution)/shard_map/routed_backward/pallas_call | solution.py:402
  65.9 3.9 %widen.1 = (f32[128,2048]{1,0:T(8,128)}, f32[128,2048]{1,0:T(8,128)}, f32[128,2048]{1,0:T(8,128)}, f32[256]{0:T(256)}) custom-call(bf16[128,2048]{1,0:T(8,128)(2,1)} %get-tuple-element.12.gq_ref, bf16[128,2048]{1,0:T(8,128)(2,1)} %get-tuple-element.13.gk_ref, bf16[128,2048]{1,0:T(8,128)(2,1)} %get-tuple-element.14.gv_ref, f32[1,256]{1,0:T(1,128)} %get-tuple-element.15.rg_ref), custom_call_target="tpu_custom_call" | custom-call | tf_op jit(solution)/shard_map/widen/pallas_call | solution.py:449

commit v3 on v2

--- a/solution.py
+++ b/solution.py
@@ -15,6 +15,12 @@
 BF16 = jnp.bfloat16
 BLOCK = 256
 NT = (((1,), (1,)), ((), ()))
+GROUPS = (
+    ((1, 0, 0), (3, 0, 0), (0, 1, 0), (2, 1, 1), (2, 0, 0)),
+    ((1, 0, 1), (3, 0, 1), (0, 1, 1), (2, 0, 1), (1, 1, 0)),
+    ((3, 1, 0), (1, 1, 1), (3, 1, 1), (2, 1, 0), (0, 0, 1)),
+)
+EVERY = GROUPS[0] + GROUPS[1] + GROUPS[2]
 CH_K, CH_Q, CH_V, CH_D, CH_LIVE, CH_W_Z, CH_W_Y, CH_DELTA, CH_TERM_Y, CH_TERM_Z, CH_SUM, CH_GQ, CH_GK, CH_GV = range(14)
 CHANNELS = 14
 
@@ -136,10 +142,10 @@
             device_id_type=MESH,
         )
 
-    def to_peers(source_of, dst, channel, axis, n, mine):
-        for o in range(1, n):
-            peer = lax.rem(mine + o, n)
-            remote(source_of(peer), dst, channel, axis, peer).start()
+    def to_peers(source_of, dst, channel, group=EVERY):
+        for dx, dz, dc in group:
+            peer = 4 * lax.rem(me // 4 + dx, n_ctx // 4) + 2 * lax.rem(me // 2 + dz, 2) + lax.rem(me + dc, 2)
+            remote(source_of(peer), dst, channel, "ctx", peer).start()
 
     def arrived(ref, channel):
         remote(ref, ref, channel, "ctx", lax.rem(me + 1, n_ctx)).wait_recv()
@@ -158,10 +164,10 @@
 
     for o in range(1, n_z):
         remote(w_all.at[me_dp], w_all.at[me_dp], CH_W_Z, "dp", z_peer(o)).start()
-    to_peers(lambda p: live_own, live_all.at[me], CH_LIVE, "ctx", n_ctx, me)
-    to_peers(lambda p: cols(k_hbm, p), kq_all.at[me, :, pl.ds(0, HEAD)], CH_K, "ctx", n_ctx, me)
-    to_peers(lambda p: cols(q_hbm, p), kq_all.at[me, :, pl.ds(HEAD, HEAD)], CH_Q, "ctx", n_ctx, me)
-    to_peers(lambda p: cols(v_hbm, p), v_all.at[me], CH_V, "ctx", n_ctx, me)
+    to_peers(lambda p: live_own, live_all.at[me], CH_LIVE)
+    to_peers(lambda p: cols(k_hbm, p), kq_all.at[me, :, pl.ds(0, HEAD)], CH_K)
+    to_peers(lambda p: cols(q_hbm, p), kq_all.at[me, :, pl.ds(HEAD, HEAD)], CH_Q)
+    to_peers(lambda p: cols(v_hbm, p), v_all.at[me], CH_V)
 
     local[1].wait()
     if n_z > 1:
@@ -191,7 +197,7 @@
         rank_row[s] = jnp.where(live_s > 0.0, before + lane, -1.0)
         before = before + jnp.sum(live_s, axis=1, keepdims=True)
 
-    to_peers(lambda p: d_send.at[p], d_all.at[me], CH_D, "ctx", n_ctx, me)
+    to_peers(lambda p: d_send.at[p], d_all.at[me], CH_D)
 
     token_row = lax.broadcasted_iota(jnp.int32, (BLOCK, rows), 0).astype(F32)
     token_lane = lax.broadcasted_iota(jnp.int32, (rows, routed), 1).astype(F32)
@@ -270,6 +276,8 @@
     for m in range(pairs):
         both = unpacked(m, gv_c, 0, HEAD).astype(BF16).reshape(per_block, rows, HEAD)
         gv_send[m * per_block : (m + 1) * per_block] = both
+
+    to_peers(lambda p: gv_send.at[p], cols(gv_ref, me), CH_GV, GROUPS[0])
 
     delta_slots = [jnp.zeros((8, rows), F32) for _ in range(n_ctx)]
     for i in range(blocks):
@@ -291,8 +299,8 @@
         delta_send[s] = jnp.sum(delta_slots[s], axis=0, keepdims=True)
     delta_all[me] = delta_send[me]
 
-    to_peers(lambda p: gv_send.at[p], cols(gv_ref, me), CH_GV, "ctx", n_ctx, me)
-    to_peers(lambda p: delta_send.at[p], delta_all.at[me], CH_DELTA, "ctx", n_ctx, me)
+    to_peers(lambda p: delta_send.at[p], delta_all.at[me], CH_DELTA)
+    to_peers(lambda p: gv_send.at[p], cols(gv_ref, me), CH_GV, GROUPS[1] + GROUPS[2])
 
     for j in range(blocks):
         rest = slice(j * BLOCK, routed)
@@ -317,14 +325,7 @@
     for o in range(1, n_y):
         group = pl.ds(lax.rem(me_y + o, n_y) * n_z, n_z)
         remote(term_send.at[group], term_y.at[me_y], CH_TERM_Y, "dp", y_peer(o)).start()
-    to_peers(lambda p: gk_send.at[p], cols(gk_ref, me), CH_GK, "ctx", n_ctx, me)
-    own = [
-        pltpu.make_async_copy(gq_send.at[me], cols(gq_ref, me), local_sem.at[5]),
-        pltpu.make_async_copy(gk_send.at[me], cols(gk_ref, me), local_sem.at[6]),
-        pltpu.make_async_copy(gv_send.at[me], cols(gv_ref, me), local_sem.at[7]),
-    ]
-    for copy in own:
-        copy.start()
+    to_peers(lambda p: gk_send.at[p], cols(gk_ref, me), CH_GK, GROUPS[0] + GROUPS[1])
     if n_y > 1:
         arrived(term_y.at[pl.ds(0, n_y - 1)], CH_TERM_Y)
     half = term_y[0]
@@ -334,6 +335,8 @@
     term_z[me_z] = term_half[me_z]
     for o in range(1, n_z):
         remote(term_half.at[lax.rem(me_z + o, n_z)], term_z.at[me_z], CH_TERM_Z, "dp", z_peer(o)).start()
+    to_peers(lambda p: gk_send.at[p], cols(gk_ref, me), CH_GK, GROUPS[2])
+    to_peers(lambda p: gq_send.at[p], cols(gq_ref, me), CH_GQ, GROUPS[0])
     if n_z > 1:
         arrived(term_z.at[pl.ds(0, n_z - 1)], CH_TERM_Z)
     term_sum = term_z[0]
@@ -341,8 +344,15 @@
         term_sum += term_z[p]
     sum_send[...] = term_sum
     sum_all[me] = term_sum
-    to_peers(lambda p: sum_send, sum_all.at[me], CH_SUM, "ctx", n_ctx, me)
-    to_peers(lambda p: gq_send.at[p], cols(gq_ref, me), CH_GQ, "ctx", n_ctx, me)
+    to_peers(lambda p: sum_send, sum_all.at[me], CH_SUM)
+    to_peers(lambda p: gq_send.at[p], cols(gq_ref, me), CH_GQ, GROUPS[1] + GROUPS[2])
+    own = [
+        pltpu.make_async_copy(gq_send.at[me], cols(gq_ref, me), local_sem.at[5]),
+        pltpu.make_async_copy(gk_send.at[me], cols(gk_ref, me), local_sem.at[6]),
+        pltpu.make_async_copy(gv_send.at[me], cols(gv_ref, me), local_sem.at[7]),
+    ]
+    for copy in own:
+        copy.start()
     arrived(sum_all.at[few], CH_SUM)
     everything = sum_all[0]
     for c in range(1, n_ctx):

time: 69.9 us -> 64.2 us (0.918)
  Pallas kernels: 69.1 us -> 63.4 us
    pallas_call x1, Pallas kernels: 65.2 us -> 59.5 us  [body(): pl.pallas_call(functools.partial(kernel, n_ctx, n_y, n_z), out_shape=(out...]
where the time goes in v3:
time: 64.2 us; the launch traced here: 64.1 us
  Pallas kernels  63.4 us (99%)
    pallas_call x1, Pallas kernels, body(): pl.pallas_call(functools.partial(kernel, n_ctx, n_y, n_z), out_shape=(out...  59.5 us
    pallas_call x1, Pallas kernels, body(): pl.pallas_call(widen, grid=(steps,), out_shape=(wide, wide, wide, jax.Sha...  3.91 us

profile of v3, /device:TPU:1, one launch (start us, length us, event | category | flops | bytes accessed | tf_op | source)
XLA Modules:
  0.0 64.1 jit_solution(13831078941273601887)
XLA Ops:
  0.6 59.5 %routed_backward.1 = (bf16[128,2048]{1,0:T(8,128)(2,1)}, bf16[128,2048]{1,0:T(8,128)(2,1)}, bf16[128,2048]{1,0:T(8,128)(2,1)}, f32[1,256]{1,0:T(1,128)}) custom-call(s32[1,128]{1,0:T(1,128)} %pos_ref.1, bf16[256]{0:T(256)(128)(2,1)} %w_ref.1, bf16[128,4096]{1,0:T(8,128)(2,1)} %bitcast.8, bf16[128,2048]{1,0:T(8,128)(2,1)} %bitcast.10, ...), custom_call_target="tpu_custom_call" | custom-call | tf_op jit(solution)/shard_map/routed_backward/pallas_call | solution.py:412
  60.2 3.9 %widen.1 = (f32[128,2048]{1,0:T(8,128)}, f32[128,2048]{1,0:T(8,128)}, f32[128,2048]{1,0:T(8,128)}, f32[256]{0:T(256)}) custom-call(bf16[128,2048]{1,0:T(8,128)(2,1)} %get-tuple-element.12.gq_ref, bf16[128,2048]{1,0:T(8,128)(2,1)} %get-tuple-element.13.gk_ref, bf16[128,2048]{1,0:T(8,128)(2,1)} %get-tuple-element.14.gv_ref, f32[1,256]{1,0:T(1,128)} %get-tuple-element.15.rg_ref), custom_call_target="tpu_custom_call" | custom-call | tf_op jit(solution)/shard_map/widen/pallas_call | solution.py:459

commit v4 on v3

--- a/solution.py
+++ b/solution.py
@@ -167,7 +167,7 @@
     to_peers(lambda p: live_own, live_all.at[me], CH_LIVE)
     to_peers(lambda p: cols(k_hbm, p), kq_all.at[me, :, pl.ds(0, HEAD)], CH_K)
     to_peers(lambda p: cols(q_hbm, p), kq_all.at[me, :, pl.ds(HEAD, HEAD)], CH_Q)
-    to_peers(lambda p: cols(v_hbm, p), v_all.at[me], CH_V)
+    to_peers(lambda p: cols(v_hbm, p), v_all.at[me], CH_V, GROUPS[0])
 
     local[1].wait()
     if n_z > 1:
@@ -198,6 +198,7 @@
         before = before + jnp.sum(live_s, axis=1, keepdims=True)
 
     to_peers(lambda p: d_send.at[p], d_all.at[me], CH_D)
+    to_peers(lambda p: cols(v_hbm, p), v_all.at[me], CH_V, GROUPS[1] + GROUPS[2])
 
     token_row = lax.broadcasted_iota(jnp.int32, (BLOCK, rows), 0).astype(F32)
     token_lane = lax.broadcasted_iota(jnp.int32, (rows, routed), 1).astype(F32)
@@ -253,11 +254,6 @@
         for j in range(i + 1):
             p_buf[span(j), span(i)] = (parts[j] * inverse).astype(BF16)
 
-    local[4].wait()
-    arrived(v_all.at[few], CH_V)
-    for b in range(blocks):
-        v_c[span(b)] = packed(v_all, b)
-
     arrived(d_all.at[few], CH_D)
     for b in range(blocks):
         d_c[span(b)] = packed(d_all, b)
@@ -277,7 +273,12 @@
         both = unpacked(m, gv_c, 0, HEAD).astype(BF16).reshape(per_block, rows, HEAD)
         gv_send[m * per_block : (m + 1) * per_block] = both
 
-    to_peers(lambda p: gv_send.at[p], cols(gv_ref, me), CH_GV, GROUPS[0])
+    to_peers(lambda p: gv_send.at[p], cols(gv_ref, me), CH_GV, GROUPS[0] + GROUPS[1])
+
+    local[4].wait()
+    arrived(v_all.at[few], CH_V)
+    for b in range(blocks):
+        v_c[span(b)] = packed(v_all, b)
 
     delta_slots = [jnp.zeros((8, rows), F32) for _ in range(n_ctx)]
     for i in range(blocks):
@@ -300,7 +301,7 @@
     delta_all[me] = delta_send[me]
 
     to_peers(lambda p: delta_send.at[p], delta_all.at[me], CH_DELTA)
-    to_peers(lambda p: gv_send.at[p], cols(gv_ref, me), CH_GV, GROUPS[1] + GROUPS[2])
+    to_peers(lambda p: gv_send.at[p], cols(gv_ref, me), CH_GV, GROUPS[2])
 
     for j in range(blocks):
         rest = slice(j * BLOCK, routed)
@@ -312,6 +313,8 @@
         both = unpacked(m, gkq_c, 0, 2 * HEAD).astype(BF16)
         gk_send[m * per_block : (m + 1) * per_block] = both[:, 0:HEAD].reshape(per_block, rows, HEAD)
         gq_send[m * per_block : (m + 1) * per_block] = both[:, HEAD : 2 * HEAD].reshape(per_block, rows, HEAD)
+
+    to_peers(lambda p: gk_send.at[p], cols(gk_ref, me), CH_GK, GROUPS[0] + GROUPS[1])
 
     arrived(delta_all.at[few], CH_DELTA)
     row_sum = delta_all[0]
@@ -325,7 +328,7 @@
     for o in range(1, n_y):
         group = pl.ds(lax.rem(me_y + o, n_y) * n_z, n_z)
         remote(term_send.at[group], term_y.at[me_y], CH_TERM_Y, "dp", y_peer(o)).start()
-    to_peers(lambda p: gk_send.at[p], cols(gk_ref, me), CH_GK, GROUPS[0] + GROUPS[1])
+    to_peers(lambda p: gk_send.at[p], cols(gk_ref, me), CH_GK, GROUPS[2])
     if n_y > 1:
         arrived(term_y.at[pl.ds(0, n_y - 1)], CH_TERM_Y)
     half = term_y[0]
@@ -335,8 +338,7 @@
     term_z[me_z] = term_half[me_z]
     for o in range(1, n_z):
         remote(term_half.at[lax.rem(me_z + o, n_z)], term_z.at[me_z], CH_TERM_Z, "dp", z_peer(o)).start()
-    to_peers(lambda p: gk_send.at[p], cols(gk_ref, me), CH_GK, GROUPS[2])
-    to_peers(lambda p: gq_send.at[p], cols(gq_ref, me), CH_GQ, GROUPS[0])
+    to_peers(lambda p: gq_send.at[p], cols(gq_ref, me), CH_GQ, GROUPS[0] + GROUPS[1])
     if n_z > 1:
         arrived(term_z.at[pl.ds(0, n_z - 1)], CH_TERM_Z)
     term_sum = term_z[0]
@@ -345,7 +347,7 @@
     sum_send[...] = term_sum
     sum_all[me] = term_sum
     to_peers(lambda p: sum_send, sum_all.at[me], CH_SUM)
-    to_peers(lambda p: gq_send.at[p], cols(gq_ref, me), CH_GQ, GROUPS[1] + GROUPS[2])
+    to_peers(lambda p: gq_send.at[p], cols(gq_ref, me), CH_GQ, GROUPS[2])
     own = [
         pltpu.make_async_copy(gq_send.at[me], cols(gq_ref, me), local_sem.at[5]),
         pltpu.make_async_copy(gk_send.at[me], cols(gk_ref, me), local_sem.at[6]),

time: 64.2 us -> 61 us (0.950)
  Pallas kernels: 63.4 us -> 60.2 us
    pallas_call x1, Pallas kernels: 59.5 us -> 56.3 us  [body(): pl.pallas_call(functools.partial(kernel, n_ctx, n_y, n_z), out_shape=(out...]
where the time goes in v4:
time: 61 us; the launch traced here: 60.9 us
  Pallas kernels  60.2 us (99%)
  between operations  0.64 us (1%)
    pallas_call x1, Pallas kernels, body(): pl.pallas_call(functools.partial(kernel, n_ctx, n_y, n_z), out_shape=(out...  56.3 us
    pallas_call x1, Pallas kernels, body(): pl.pallas_call(widen, grid=(steps,), out_shape=(wide, wide, wide, jax.Sha...  3.91 us

profile of v4, /device:TPU:1, one launch (start us, length us, event | category | flops | bytes accessed | tf_op | source)
XLA Modules:
  0.0 60.9 jit_solution(2171922261975764650)
XLA Ops:
  0.6 56.3 %routed_backward.1 = (bf16[128,2048]{1,0:T(8,128)(2,1)}, bf16[128,2048]{1,0:T(8,128)(2,1)}, bf16[128,2048]{1,0:T(8,128)(2,1)}, f32[1,256]{1,0:T(1,128)}) custom-call(s32[1,128]{1,0:T(1,128)} %pos_ref.1, bf16[256]{0:T(256)(128)(2,1)} %w_ref.1, bf16[128,4096]{1,0:T(8,128)(2,1)} %bitcast.8, bf16[128,2048]{1,0:T(8,128)(2,1)} %bitcast.10, ...), custom_call_target="tpu_custom_call" | custom-call | tf_op jit(solution)/shard_map/routed_backward/pallas_call | solution.py:414
  57.0 3.9 %widen.1 = (f32[128,2048]{1,0:T(8,128)}, f32[128,2048]{1,0:T(8,128)}, f32[128,2048]{1,0:T(8,128)}, f32[256]{0:T(256)}) custom-call(bf16[128,2048]{1,0:T(8,128)(2,1)} %get-tuple-element.12.gq_ref, bf16[128,2048]{1,0:T(8,128)(2,1)} %get-tuple-element.13.gk_ref, bf16[128,2048]{1,0:T(8,128)(2,1)} %get-tuple-element.14.gv_ref, f32[1,256]{1,0:T(1,128)} %get-tuple-element.15.rg_ref), custom_call_target="tpu_custom_call" | custom-call | tf_op jit(solution)/shard_map/widen/pallas_call | solution.py:461

commit v5 on v4

--- a/solution.py
+++ b/solution.py
@@ -455,7 +455,7 @@
         compiler_params=pltpu.CompilerParams(collective_id=0, has_side_effects=True, vmem_limit_bytes=60 * 1024 * 1024),
         name="routed_backward",
     )(route_pos, w_router, x_routed[0], queries[0], keys[0], values[0], d_gated[0])
-    steps = 4
+    steps = 2
     tile = pl.BlockSpec((rows // steps, width), lambda i: (i, 0))
     wide = jax.ShapeDtypeStruct((rows, width), F32)
     gq, gk, gv, rg = pl.pallas_call(

time: 61 us -> 59.9 us (0.982)
  Pallas kernels: 60.2 us -> 59.2 us
    pallas_call x1, Pallas kernels: 3.91 us -> 2.85 us  [body(): pl.pallas_call(widen, grid=(steps,), out_shape=(wide, wide, wide, jax.Sha...]
where the time goes in v5:
time: 59.9 us; the launch traced here: 59.8 us
  Pallas kernels  59.2 us (99%)
  between operations  0.64 us (1%)
    pallas_call x1, Pallas kernels, body(): pl.pallas_call(functools.partial(kernel, n_ctx, n_y, n_z), out_shape=(out...  56.3 us
    pallas_call x1, Pallas kernels, body(): pl.pallas_call(widen, grid=(steps,), out_shape=(wide, wide, wide, jax.Sha...  2.85 us

profile of v5, /device:TPU:1, one launch (start us, length us, event | category | flops | bytes accessed | tf_op | source)
XLA Modules:
  0.0 59.8 jit_solution(3573832360542372419)
XLA Ops:
  0.6 56.3 %routed_backward.1 = (bf16[128,2048]{1,0:T(8,128)(2,1)}, bf16[128,2048]{1,0:T(8,128)(2,1)}, bf16[128,2048]{1,0:T(8,128)(2,1)}, f32[1,256]{1,0:T(1,128)}) custom-call(s32[1,128]{1,0:T(1,128)} %pos_ref.1, bf16[256]{0:T(256)(128)(2,1)} %w_ref.1, bf16[128,4096]{1,0:T(8,128)(2,1)} %bitcast.8, bf16[128,2048]{1,0:T(8,128)(2,1)} %bitcast.10, ...), custom_call_target="tpu_custom_call" | custom-call | tf_op jit(solution)/shard_map/routed_backward/pallas_call | solution.py:414
  57.0 2.9 %widen.1 = (f32[128,2048]{1,0:T(8,128)}, f32[128,2048]{1,0:T(8,128)}, f32[128,2048]{1,0:T(8,128)}, f32[256]{0:T(256)}) custom-call(bf16[128,2048]{1,0:T(8,128)(2,1)} %get-tuple-element.12.gq_ref, bf16[128,2048]{1,0:T(8,128)(2,1)} %get-tuple-element.13.gk_ref, bf16[128,2048]{1,0:T(8,128)(2,1)} %get-tuple-element.14.gv_ref, f32[1,256]{1,0:T(1,128)} %get-tuple-element.15.rg_ref), custom_call_target="tpu_custom_call" | custom-call | tf_op jit(solution)/shard_map/widen/pallas_call | solution.py:461

commit v6 on v5

--- a/solution.py
+++ b/solution.py
@@ -16,9 +16,9 @@
 BLOCK = 256
 NT = (((1,), (1,)), ((), ()))
 GROUPS = (
-    ((1, 0, 0), (3, 0, 0), (0, 1, 0), (2, 1, 1), (2, 0, 0)),
-    ((1, 0, 1), (3, 0, 1), (0, 1, 1), (2, 0, 1), (1, 1, 0)),
-    ((3, 1, 0), (1, 1, 1), (3, 1, 1), (2, 1, 0), (0, 0, 1)),
+    ((2, 0, 0), (3, 1, 1), (1, 1, 0), (2, 1, 0), (0, 0, 1)),
+    ((2, 1, 1), (1, 0, 0), (3, 0, 0), (0, 1, 0), (1, 1, 1)),
+    ((2, 0, 1), (1, 0, 1), (3, 0, 1), (0, 1, 1), (3, 1, 0)),
 )
 EVERY = GROUPS[0] + GROUPS[1] + GROUPS[2]
 CH_K, CH_Q, CH_V, CH_D, CH_LIVE, CH_W_Z, CH_W_Y, CH_DELTA, CH_TERM_Y, CH_TERM_Z, CH_SUM, CH_GQ, CH_GK, CH_GV = range(14)

time: 59.9 us -> 59.5 us (level)
  no operation moved by 1% of the time
where the time goes in v6:
time: 59.5 us; the launch traced here: 59.4 us
  Pallas kernels  58.8 us (99%)
  between operations  0.64 us (1%)
    pallas_call x1, Pallas kernels, body(): pl.pallas_call(functools.partial(kernel, n_ctx, n_y, n_z), out_shape=(out...  55.9 us
    pallas_call x1, Pallas kernels, body(): pl.pallas_call(widen, grid=(steps,), out_shape=(wide, wide, wide, jax.Sha...  2.85 us

profile of v6, /device:TPU:1, one launch (start us, length us, event | category | flops | bytes accessed | tf_op | source)
XLA Modules:
  0.0 59.4 jit_solution(17711443104498233220)
XLA Ops:
  0.6 55.9 %routed_backward.1 = (bf16[128,2048]{1,0:T(8,128)(2,1)}, bf16[128,2048]{1,0:T(8,128)(2,1)}, bf16[128,2048]{1,0:T(8,128)(2,1)}, f32[1,256]{1,0:T(1,128)}) custom-call(s32[1,128]{1,0:T(1,128)} %pos_ref.1, bf16[256]{0:T(256)(128)(2,1)} %w_ref.1, bf16[128,4096]{1,0:T(8,128)(2,1)} %bitcast.8, bf16[128,2048]{1,0:T(8,128)(2,1)} %bitcast.10, ...), custom_call_target="tpu_custom_call" | custom-call | tf_op jit(solution)/shard_map/routed_backward/pallas_call | solution.py:414
  56.5 2.9 %widen.1 = (f32[128,2048]{1,0:T(8,128)}, f32[128,2048]{1,0:T(8,128)}, f32[128,2048]{1,0:T(8,128)}, f32[256]{0:T(256)}) custom-call(bf16[128,2048]{1,0:T(8,128)(2,1)} %get-tuple-element.12.gq_ref, bf16[128,2048]{1,0:T(8,128)(2,1)} %get-tuple-element.13.gk_ref, bf16[128,2048]{1,0:T(8,128)(2,1)} %get-tuple-element.14.gv_ref, f32[1,256]{1,0:T(1,128)} %get-tuple-element.15.rg_ref), custom_call_target="tpu_custom_call" | custom-call | tf_op jit(solution)/shard_map/widen/pallas_call | solution.py:461
